TPU v7x, 256 devices: a whole 4x4x8 slice. The times are simulated.
256 devices in a mesh: wall: 2 (over z_lo), plane: 128 (over x, y, z_hi, core).
Axes of the slice: x: 4, y: 4, z: 8 (z_hi: 4, z_lo: 2; z = z_hi * 2 + z_lo), core: 2. Of those that a mesh axis runs over, the one named last changes fastest.
Arguments:
- jacobian: float32 [3, 16, 16, 32, 128, 128], P(None, None, None, 'wall', 'plane'), as said below
- residual: float32 [16, 32, 128, 128], P(None, 'wall', 'plane')
- previous_update: float32 [16, 32, 128, 128], P(None, 'wall', 'plane'), may hold values from -6 to 6
- offline_coupling: float32 [4, 16, 32, 128, 128], P(None, None, 'wall', 'plane'), may hold values from 0.003 to 0.03
- wake_partner: int32 [128, 128], P('plane'), may hold values from 0 to 127, each once within a row
- line_length: int32 [128, 128], P('plane'), may hold values from 16 to 32
- bottom_flag: int32 [128, 128], P('plane'), may hold values 0 or 1
Outputs:
- update: float32 [16, 32, 128, 128], P(None, 'wall', 'plane')
Inputs may be any that keep to these rules, and one draw needn't show every extreme that they name: jacobian[2, :, :, k] is the transpose of jacobian[0, :, :, k + 1], every jacobian[1, :, :, k] is symmetric, and every row of a line's matrix is strictly diagonally dominant with a positive diagonal. `bottom_flag`: 1 where a column's first cell lies on the wake cut, 0 where it lies on the capsule wall. `wake_partner`: for a wake-cut column (i, j), the spanwise index of the column at station (i + 64) modulo 128, on the other branch of the cut, that lies beneath its first cell; each row is a permutation of 0 to 127.
All inputs are finite; a program needn't handle non-finite values. No bound on the sum of `bottom_flag` on one device may be relied on, other than what follows from the above.
Results may differ from a plain program's by a relative error of at most 0.0003.
Values sent between devices are 32-bit elements; how exact they have to be, the bound alone decides.
No kernel may reach another device: no remote copies, remote signals or barrier semaphores. Data moves between devices by JAX's collectives and lax.ppermute only.
A program may use at most 192 MiB of HBM per device.

v0:
```python
import jax
import jax.numpy as jnp
from jax import lax
from jax.sharding import PartitionSpec as P

precise = lax.Precision.HIGHEST


def with_halo(block, sides, width):
    for axis, dim in sides:
        count = lax.axis_size(axis)
        forward = [(i, i + 1) for i in range(count - 1)]
        backward = [(target, source) for source, target in forward]
        low = lax.ppermute(
            lax.slice_in_dim(block, block.shape[dim] - width, None, axis=dim), axis, forward
        )
        high = lax.ppermute(lax.slice_in_dim(block, 0, width, axis=dim), axis, backward)
        block = jnp.concatenate([low, block, high], axis=dim)
    return block


def from_behind(block, axis, distance):
    devices = range(lax.axis_size(axis))
    route = [(i - distance, i) for i in devices if i - distance in devices]
    return lax.ppermute(block, axis, route)


def product(left, right):
    return jnp.einsum("vwc,wuc->vuc", left, right, precision=precise)


def solve_block(matrix, given):
    extent = matrix.shape[0]
    augmented = jnp.concatenate([matrix, given], axis=1)
    for pivot in range(extent):
        pivot_row = augmented[pivot] / augmented[pivot, pivot][None, :]
        augmented = augmented - augmented[:, pivot][:, None, :] * pivot_row[None]
        augmented = augmented.at[pivot].set(pivot_row)
    return augmented[:, extent:]


def effective(lower, middle, upper, active_here, active_above, not_bottom):
    identity = jnp.eye(lower.shape[0], dtype=jnp.float32)[:, :, None, None]
    return (
        lower * (active_here * not_bottom)[None, None],
        middle * active_here[None, None] + identity * (1.0 - active_here)[None, None],
        upper * active_above[None, None],
    )


def eliminate(lower, middle, upper, source, block_in, vector_in, levels):
    extent = lower.shape[0]
    blocks = jnp.zeros(lower.shape, jnp.float32)
    vectors = jnp.zeros(source.shape, jnp.float32)

    def advance(level, state):
        block_prev, vector_prev, blocks, vectors = state
        below = lax.dynamic_index_in_dim(lower, level, 2, keepdims=False)
        centre = lax.dynamic_index_in_dim(middle, level, 2, keepdims=False)
        above = lax.dynamic_index_in_dim(upper, level, 2, keepdims=False)
        given = lax.dynamic_index_in_dim(source, level, 2, keepdims=False)
        schur = centre - product(below, block_prev)
        reduced = given - product(below, vector_prev)
        joined = solve_block(schur, jnp.concatenate([above, reduced], axis=1))
        block_next = joined[:, :extent]
        vector_next = joined[:, extent:]
        blocks = lax.dynamic_update_index_in_dim(blocks, block_next, level, 2)
        vectors = lax.dynamic_update_index_in_dim(vectors, vector_next, level, 2)
        return (block_next, vector_next, blocks, vectors)

    return lax.fori_loop(0, levels, advance, (block_in, vector_in, blocks, vectors))


def substitute(blocks, vectors, value_above, levels, result):

    def retreat(count, state):
        value_next, result = state
        level = levels - 1 - count
        block = lax.dynamic_index_in_dim(blocks, level, 2, keepdims=False)
        vector = lax.dynamic_index_in_dim(vectors, level, 2, keepdims=False)
        value = vector - product(block, value_next)
        result = lax.dynamic_update_index_in_dim(result, value, level, 2)
        return (value, result)

    return lax.fori_loop(0, levels, retreat, (value_above, result))


def per_device(
    jacobian, residual, previous_update, offline_coupling, wake_partner, line_length, bottom_flag
):
    unknowns = jacobian.shape[1]
    depth = jacobian.shape[3]
    stations = jacobian.shape[4]
    span = jacobian.shape[5]
    columns = stations * span
    wall_index = lax.axis_index("wall")
    plane_index = lax.axis_index("plane")
    planes = lax.axis_size("plane")
    padded = with_halo(previous_update, (("plane", 2),), 1)
    offline = (
        offline_coupling[0] * padded[:, :, :-2]
        + offline_coupling[1] * padded[:, :, 2:]
        + offline_coupling[2] * jnp.roll(previous_update, 1, axis=3)
        + offline_coupling[3] * jnp.roll(previous_update, -1, axis=3)
    )
    bottom_row = previous_update[:, 0]
    mirror_index = (plane_index + planes // 2) % planes
    whole = lax.all_gather(bottom_row, "plane", axis=1, tiled=True)
    facing = lax.dynamic_slice_in_dim(whole, mirror_index * stations, stations, 1)
    partner = jnp.take_along_axis(facing, wake_partner[None], axis=2)
    weight = bottom_flag.astype(jnp.float32) * (wall_index == 0).astype(jnp.float32)
    wake = (
        jnp.einsum("vwij,wij->vij", jacobian[0, :, :, 0], partner, precision=precise) * weight[None]
    )
    levels = wall_index * depth + jnp.arange(depth, dtype=jnp.int32)
    active = (levels[:, None, None] < line_length[None]).astype(jnp.float32)
    active_above = ((levels + 1)[:, None, None] < line_length[None]).astype(jnp.float32)
    not_bottom = (levels > 0).astype(jnp.float32)[:, None]
    source = residual + offline
    source = source.at[:, 0].add(-wake)
    source = (source * active[None]).reshape(unknowns, 1, depth, columns)
    blocks = jacobian.reshape(3, unknowns, unknowns, depth, columns)
    lower, middle, upper = effective(
        blocks[0],
        blocks[1],
        blocks[2],
        active.reshape(depth, columns),
        active_above.reshape(depth, columns),
        not_bottom,
    )
    empty_block = jnp.zeros((unknowns, unknowns, columns), jnp.float32)
    empty_vector = jnp.zeros((unknowns, 1, columns), jnp.float32)
    block_in = empty_block
    vector_in = empty_vector
    parts = eliminate(lower, middle, upper, source, block_in, vector_in, depth)
    handed = from_behind(
        jnp.concatenate([parts[2][:, :, depth - 1], parts[3][:, :, depth - 1]], axis=1), "wall", 1
    )
    block_in = handed[:, :unknowns]
    vector_in = handed[:, unknowns:]
    parts = eliminate(lower, middle, upper, source, block_in, vector_in, depth)
    value_above = empty_vector
    solved = substitute(
        parts[2], parts[3], value_above, depth, jnp.zeros(source.shape, jnp.float32)
    )
    value_above = from_behind(solved[1][:, :, 0], "wall", -1)
    solution = substitute(
        parts[2], parts[3], value_above, depth, jnp.zeros(source.shape, jnp.float32)
    )[1]
    return solution[:, 0].reshape(unknowns, depth, stations, span)


def solution(mesh):
    return jax.shard_map(
        per_device,
        mesh=mesh,
        in_specs=(
            P(None, None, None, "wall", "plane", None),
            P(None, "wall", "plane", None),
            P(None, "wall", "plane", None),
            P(None, None, "wall", "plane", None),
            P("plane", None),
            P("plane", None),
            P("plane", None),
        ),
        out_specs=P(None, "wall", "plane", None),
        check_vma=False,
    )
```

profile of v0, /device:TPU:1, one launch (start us, length us, event | category | flops | bytes accessed | tf_op | source)
XLA Modules:
  0.0 605.0 jit_solution(280235571044377390)
XLA Ops:
  7.5 6.3 %collective-permute-start = (f32[16,16,1,128]{3,0,1,2:T(8,128)S(1)}, f32[16,16,1,128]{3,0,1,2:T(8,128)S(1)}, u32[]{:S(2)}, u32[]{:S(2)}) collective-permute-start(f32[16,16,1,128]{3,0,1,2:T(8,128)S(1)} %copy.131), channel_id=1, source_target_pairs={{0,1},{1,2},{2,3},{3,4},{4,5},{5,6},{6,7},{7,8},{8,9},{9,10},{10,1... | collective-permute-start | bytes 393224 | tf_op jit(solution)/shard_map/ppermute | solution.py:14
  22.3 8.3 %fusion.22 = (f32[1,16,16,16,1,128]{5,4,3,2,1,0:T(1,128)}, f32[1,16,16,16,1,128]{5,4,3,2,1,0:T(1,128)}, f32[1,16,16,16,1,128]{5,4,3,2,1,0:T(1,128)S(1)}) fusion(f32[3,16,16,16,1,128]{5,4,3,2,1,0:T(1,128)} %param.81), kind=kLoop, calls=%fused_computation.232 | loop fusion | bytes 12582912 | tf_op jit(solution)/shard_map/slice | solution.py:126
  30.6 12.0 %copy.215 = f32[1,16,16,16,1,128]{2,1,5,3,4,0:T(8,128)} copy(f32[1,16,16,16,1,128]{5,4,3,2,1,0:T(1,128)} %get-tuple-element.1768) | data formatting | bytes 4194304
  42.6 10.7 %copy.216 = f32[1,16,16,16,1,128]{2,1,5,3,4,0:T(8,128)} copy(f32[1,16,16,16,1,128]{5,4,3,2,1,0:T(1,128)S(1)} %get-tuple-element.1769) | data formatting | bytes 4194304
  57.6 15.1 %fusion.10 = f32[16,16,16,128]{1,0,3,2:T(8,128)} fusion(f32[1,16,16,16,1,128]{2,1,5,3,4,0:T(8,128)} %copy.215, f32[16,128]{1,0:T(8,128)S(1)} %copy-done.3, f32[16,16]{1,0:T(8,128)S(1)} %fusion.20, f32[16,128]{1,0:T(8,128)S(1)} %get-tuple-element.1781), kind=kLoop, calls=%fused_computation.191 | loop fusion | flops 1572864 | bytes 4211712 | tf_op jit(solution)/shard_map/add | solution.py:46
  72.8 6.5 %bitcast_multiply_fusion.2 = f32[16,16,16,128]{1,0,3,2:T(8,128)} fusion(f32[1,16,16,16,1,128]{2,1,5,3,4,0:T(8,128)S(1)} %bitcast.632, f32[16,128]{1,0:T(8,128)S(1)} %copy-done.2), kind=kLoop, calls=%fused_computation.189 | loop fusion | flops 524288 | bytes 4202496 | tf_op jit(solution)/shard_map/mul | solution.py:45
  80.5 23.8 %all-gather.3.cloned.1.call-done = f32[16,128,1,128]{3,2,1,0:T(1,128)} async-done(((f32[16,1,1,128]{3,2,1,0:T(1,128)}), f32[16,128,1,128]{3,2,1,0:T(1,128)}) %all-gather.3.cloned.1.call-update) | async-done | bytes 1048592 | tf_op jit(solution)/shard_map/all_gather | solution.py:108
  106.0 185.2 %while.112 = (s32[]{:T(128)}, f32[16,16,128]{2,0,1:T(8,128)S(1)}, f32[16,1,128]{2,0,1:T(8,128)S(1)}, f32[16,16,16,128]{3,0,1,2:T(8,128)}, f32[16,1,16,128]{3,0,2...) while((s32[]{:T(128)}, f32[16,16,128]{2,0,1:T(8,128)S(1)}, ...), condition=%wide.region_1.2_spmd, body=%wide.region_0.1_spmd.sunk | while | flops 8890370 | bytes 15271725 | solution.py:71
  296.7 249.2 %while.113 = (s32[]{:T(128)}, f32[16,16,128]{2,0,1:T(8,128)S(1)}, f32[16,1,128]{2,0,1:T(8,128)S(1)}, f32[16,16,16,128]{3,2,1,0:T(8,128)}, f32[16,1,16,128]{3,0,2...) while((s32[]{:T(128)}, f32[16,16,128]{2,0,1:T(8,128)S(1)}, ...), condition=%wide.region_3.4_spmd, body=%wide.region_2.3_spmd.sunk | while | flops 8890370 | bytes 15926577 | solution.py:71
  338.8 4.5 dynamic_update_slice.80
  354.4 4.5 dynamic_update_slice.80
  369.9 4.5 dynamic_update_slice.80
  385.5 4.5 dynamic_update_slice.80
  401.0 4.5 dynamic_update_slice.80
  432.2 4.5 dynamic_update_slice.80
  447.8 4.5 dynamic_update_slice.80
  463.4 4.5 dynamic_update_slice.80
  479.0 4.5 dynamic_update_slice.80
  494.6 4.5 dynamic_update_slice.80
  510.2 4.5 dynamic_update_slice.80
  525.8 4.5 dynamic_update_slice.80
  541.4 4.5 dynamic_update_slice.80
  545.9 23.7 %while.115 = (s32[]{:T(128)}, f32[16,1,128]{2,0,1:T(8,128)S(1)}, f32[16,1,16,128]{3,2,1,0:T(8,128)S(1)}, f32[16,1,16,128]{3,0,2,1:T(8,128)S(1)}, f32[16,16,16,12...) while((s32[]{:T(128)}, f32[16,1,128]{2,0,1:T(8,128)S(1)}, ...), condition=%wide.region_5.6_spmd.clone, body=%wide.region_4.5_spmd.clone.sunk | while | flops 67591 | bytes 467105 | solution.py:85
  574.1 23.4 %while.114 = (s32[]{:T(128)}, f32[16,1,128]{2,0,1:T(8,128)S(1)}, f32[16,1,16,128]{3,2,1,0:T(8,128)S(1)}, f32[16,1,16,128]{3,0,2,1:T(8,128)S(1)}, f32[16,16,16,12...) while((s32[]{:T(128)}, f32[16,1,128]{2,0,1:T(8,128)S(1)}, ...), condition=%wide.region_7.8_spmd, body=%wide.region_6.7_spmd.sunk | while | flops 65542 | bytes 450711 | solution.py:85
  (3677 shorter events, 426.8 us)
Async XLA Ops:
  6.5 14.4 %copy-start.4 = (s32[1,128]{1,0:T(1,128)S(1)}, s32[1,128]{1,0:T(1,128)}, u32[]{:S(2)}) copy-start(s32[1,128]{1,0:T(1,128)} %param.86) | copy-start | bytes 1540
  6.5 97.8 %all-gather.3.cloned.1.call-start = ((), (), s32[]{:S(2)}) async-start(), calls=%async_computation | async-start | bytes 1056768 | tf_op jit(solution)/shard_map/all_gather | solution.py:108
  7.5 72.7 %collective-permute-start = (f32[16,16,1,128]{3,0,1,2:T(8,128)S(1)}, f32[16,16,1,128]{3,0,1,2:T(8,128)S(1)}, u32[]{:S(2)}, u32[]{:S(2)}) collective-permute-start(f32[16,16,1,128]{3,0,1,2:T(8,128)S(1)} %copy.131), channel_id=1, source_target_pairs={{0,1},{1,2},{2,3},{3,4},{4,5},{5,6},{6,7},{7,8},{8,9},{9,10},{10,1... | collective-permute-start | bytes 393224 | tf_op jit(solution)/shard_map/ppermute | solution.py:14
  13.8 66.4 %collective-permute-start.1 = (f32[16,16,1,128]{3,0,1,2:T(8,128)S(1)}, f32[16,16,1,128]{3,0,1,2:T(8,128)S(1)}, u32[]{:S(2)}, u32[]{:S(2)}) collective-permute-start(f32[16,16,1,128]{3,0,1,2:T(8,128)S(1)} %copy.131), channel_id=1, source_target_pairs={{1,0},{2,1},{3,2},{4,3},{5,4},{6,5},{7,6},{8,7},{9,8},{10,9},{11,1... | collective-permute-start | bytes 393224 | tf_op jit(solution)/shard_map/ppermute | solution.py:17
  53.3 4.3 copy-start.3
  53.3 19.4 %slice-start = ((s8[16777216]{0:T(1024)(128)(4,1)}), s8[4194304]{0:T(1024)(128)(4,1)S(1)}, s32[]{:S(2)}) async-start(s8[16777216]{0:T(1024)(128)(4,1)} %bitcast.631), calls=%async_computation.1 | async-start | bytes 8388608
  57.6 15.1 %slice-start.1 = ((s8[16777216]{0:T(1024)(128)(4,1)}), s8[4194304]{0:T(1024)(128)(4,1)S(1)}, s32[]{:S(2)}) async-start(s8[16777216]{0:T(1024)(128)(4,1)} %bitcast.631), calls=%async_computation.2 | async-start | bytes 8388608
  57.6 15.1 %slice-start.2 = ((s8[16777216]{0:T(1024)(128)(4,1)}), s8[4194304]{0:T(1024)(128)(4,1)S(1)}, s32[]{:S(2)}) async-start(s8[16777216]{0:T(1024)(128)(4,1)} %bitcast.631), calls=%async_computation.3 | async-start | bytes 8388608
  57.6 15.1 %slice-start.3 = ((s8[16777216]{0:T(1024)(128)(4,1)}), s8[4194304]{0:T(1024)(128)(4,1)S(1)}, s32[]{:S(2)}) async-start(s8[16777216]{0:T(1024)(128)(4,1)} %bitcast.631), calls=%async_computation.4 | async-start | bytes 8388608
  57.6 15.1 %copy-start.2 = (f32[16,128]{1,0:T(8,128)S(1)}, f32[16,128]{1,0:T(8,128)}, u32[]{:S(2)}) copy-start(f32[16,128]{1,0:T(8,128)} %get-tuple-element.1778) | copy-start | bytes 24580
  72.7 6.5 %copy-start.7 = (s32[1,128]{1,0:T(1,128)S(1)}, s32[1,128]{1,0:T(1,128)}, u32[]{:S(2)}) copy-start(s32[1,128]{1,0:T(1,128)} %param.87) | copy-start | bytes 1540
  72.8 7.4 %copy-start.6 = (s32[128]{0:T(128)S(1)}, s32[128]{0:T(128)}, u32[]{:S(2)}) copy-start(s32[128]{0:T(128)} %fusion.21) | copy-start | bytes 1540
  72.8 7.5 %copy-start = (f32[16,16,1,128]{3,2,1,0:T(1,128)S(1)}, f32[16,16,1,128]{3,2,1,0:T(1,128)}, u32[]{:S(2)}) copy-start(f32[16,16,1,128]{3,2,1,0:T(1,128)} %param.82) | copy-start | bytes 393220
  72.8 33.0 %copy-start.5 = (pred[128]{0:T(512)(128)(4,1)S(1)}, pred[128]{0:T(512)(128)(4,1)}, u32[]{:S(2)}) copy-start(pred[128]{0:T(512)(128)(4,1)} %compare_and_fusion) | copy-start | bytes 388
  292.2 4.4 collective-permute-start.2
  569.6 4.5 collective-permute-start.3
  597.5 0.7 copy-start.1
Sparse Core Ops, SparseCore 0:
  17.2 87.0 all-gather.2
where the time goes:
time: 611 us; the launch traced here: 605 us
  local copies, waits for them, and re-layouts  330 us (54%)
  other arithmetic  110 us (18%)
  matrix products  86.9 us (14%)
  waiting for transfers between devices  30 us (5%)
  loops' own time  23.4 us (4%)
  between operations  13.8 us (2%)
  starting transfers between devices  11 us (2%)
    dot_general x32, matrix products, product(): return jnp.einsum('vwc,wuc->vuc', left, right, precision=precise)  86.9 us
    dynamic_update_slice x48, local copies, waits for them, and re-layouts, advance(): blocks = lax.dynamic_update_index_in_dim(blocks, block_next, level, 2)  84.7 us
    while x48, other arithmetic  50.4 us
    scatter x512, local copies, waits for them, and re-layouts, solve_block(): augmented = augmented.at[pivot].set(pivot_row)  44.3 us
    dynamic_slice x32, local copies, waits for them, and re-layouts, retreat(): block = lax.dynamic_index_in_dim(blocks, level, 2, keepdims=False)  42.4 us
    slice x32, local copies, waits for them, and re-layouts, solve_block(): pivot_row = augmented[pivot] / augmented[pivot, pivot][None, :]  32.9 us
    squeeze x32, local copies, waits for them, and re-layouts, advance(): above = lax.dynamic_index_in_dim(upper, level, 2, keepdims=False)  29.3 us
    unnamed x28, local copies, waits for them, and re-layouts  24.4 us
  transfers between devices with their start and end apart: 5, of which 3 were waited for; matrix products, arithmetic and copies ran while one was open for 11% of the time, Pallas kernels for 0%

commit v1 on v0

--- a/solution.py
+++ b/solution.py
@@ -105,7 +105,8 @@
     )
     bottom_row = previous_update[:, 0]
     mirror_index = (plane_index + planes // 2) % planes
-    whole = lax.all_gather(bottom_row, "plane", axis=1, tiled=True)
+    repeated = jnp.stack([bottom_row] * lax.axis_size("plane"))
+    whole = jnp.concatenate(lax.all_to_all(repeated, "plane", 0, 0), axis=1)
     facing = lax.dynamic_slice_in_dim(whole, mirror_index * stations, stations, 1)
     partner = jnp.take_along_axis(facing, wake_partner[None], axis=2)
     weight = bottom_flag.astype(jnp.float32) * (wall_index == 0).astype(jnp.float32)

time: 611 us -> 592 us (0.969)
  waiting for transfers between devices: 30 us -> 5.08 us
  starting transfers between devices: 11 us -> 28.3 us
  between operations: 13.8 us -> 0.5 us
    all_gather x1 -> x0, waiting for transfers between devices: 23.8 us -> none  [per_device(): whole = lax.all_gather(bottom_row, 'plane', axis=1, tiled=True)]
    all_to_all x0 -> x1, starting transfers between devices: none -> 16 us  [per_device(): whole = jnp.concatenate(lax.all_to_all(repeated, 'plane', 0, 0), axis=1)]
    another operation x36 -> x39, local copies, waits for them, and re-layouts: 16.9 us -> 18.1 us
    unnamed x28 -> x44, local copies, waits for them, and re-layouts: 24.4 us -> 24.5 us
  transfers between devices with their start and end apart: 5 -> 5, of which waited for: 3 -> 2; matrix products, arithmetic and copies ran while one was open for 11% -> 11% of each run, Pallas kernels for 0% -> 0%
where the time goes in v1:
time: 592 us; the launch traced here: 584 us
  local copies, waits for them, and re-layouts  330 us (56%)
  other arithmetic  110 us (19%)
  matrix products  87 us (15%)
  starting transfers between devices  28.3 us (5%)
  loops' own time  23.4 us (4%)
    dot_general x32, matrix products, product(): return jnp.einsum('vwc,wuc->vuc', left, right, precision=precise)  87 us
    dynamic_update_slice x48, local copies, waits for them, and re-layouts, advance(): blocks = lax.dynamic_update_index_in_dim(blocks, block_next, level, 2)  84.8 us
    while x48, other arithmetic  50.4 us
    scatter x512, local copies, waits for them, and re-layouts, solve_block(): augmented = augmented.at[pivot].set(pivot_row)  44.3 us
    dynamic_slice x32, local copies, waits for them, and re-layouts, retreat(): block = lax.dynamic_index_in_dim(blocks, level, 2, keepdims=False)  42.4 us
    slice x32, local copies, waits for them, and re-layouts, solve_block(): pivot_row = augmented[pivot] / augmented[pivot, pivot][None, :]  32.9 us
    squeeze x32, local copies, waits for them, and re-layouts, advance(): above = lax.dynamic_index_in_dim(upper, level, 2, keepdims=False)  29.3 us
    unnamed x44, local copies, waits for them, and re-layouts  24.5 us
  transfers between devices with their start and end apart: 5, of which 2 were waited for; matrix products, arithmetic and copies ran while one was open for 11% of the time, Pallas kernels for 0%

profile of v1, /device:TPU:1, one launch (start us, length us, event | category | flops | bytes accessed | tf_op | source)
XLA Modules:
  0.0 584.1 jit_solution(3549836393480310353)
XLA Ops:
  1.0 6.3 %collective-permute-start = (f32[16,16,1,128]{3,0,1,2:T(8,128)S(1)}, f32[16,16,1,128]{3,0,1,2:T(8,128)}, u32[]{:S(2)}, u32[]{:S(2)}) collective-permute-start(f32[16,16,1,128]{3,0,1,2:T(8,128)S(1)} %copy.131), channel_id=1, source_target_pairs={{0,1},{1,2},{2,3},{3,4},{4,5},{5,6},{6,7},{7,8},{8,9},{9,10},{10,1... | collective-permute-start | bytes 393224 | tf_op jit(solution)/shard_map/ppermute | solution.py:14
  11.0 16.0 %all-to-all-start = ((f32[128,16,1,128]{3,1,2,0:T(8,128)}), f32[128,16,1,128]{3,1,2,0:T(8,128)S(1)}, u32[]{:S(2)}, u32[]{:S(2)}) async-start(f32[128,16,1,128]{3,1,2,0:T(8,128)} %stack.3), calls=%async_computation | async-start | bytes 2097152 | tf_op jit(solution)/shard_map/all_to_all | solution.py:109
  31.0 8.3 %fusion.22 = (f32[1,16,16,16,1,128]{5,4,3,2,1,0:T(1,128)}, f32[1,16,16,16,1,128]{5,4,3,2,1,0:T(1,128)}, f32[1,16,16,16,1,128]{5,4,3,2,1,0:T(1,128)S(1)}) fusion(f32[3,16,16,16,1,128]{5,4,3,2,1,0:T(1,128)} %param.81), kind=kLoop, calls=%fused_computation.232 | loop fusion | bytes 12582912 | tf_op jit(solution)/shard_map/slice | solution.py:127
  39.4 12.0 %copy.215 = f32[1,16,16,16,1,128]{2,1,5,3,4,0:T(8,128)} copy(f32[1,16,16,16,1,128]{5,4,3,2,1,0:T(1,128)} %get-tuple-element.1768) | data formatting | bytes 4194304
  51.4 10.7 %copy.216 = f32[1,16,16,16,1,128]{2,1,5,3,4,0:T(8,128)} copy(f32[1,16,16,16,1,128]{5,4,3,2,1,0:T(1,128)S(1)} %get-tuple-element.1769) | data formatting | bytes 4194304
  66.4 15.1 %fusion.10 = f32[16,16,16,128]{1,0,3,2:T(8,128)} fusion(f32[1,16,16,16,1,128]{2,1,5,3,4,0:T(8,128)} %copy.215, f32[16,128]{1,0:T(8,128)S(1)} %copy-done.10, f32[16,16]{1,0:T(8,128)S(1)} %fusion.20, f32[16,128]{1,0:T(8,128)S(1)} %get-tuple-element.1781), kind=kLoop, calls=%fused_computation.191 | loop fusion | flops 1572864 | bytes 4211712 | tf_op jit(solution)/shard_map/add | solution.py:46
  81.6 6.4 %bitcast_multiply_fusion.2 = f32[16,16,16,128]{1,0,3,2:T(8,128)} fusion(f32[1,16,16,16,1,128]{2,1,5,3,4,0:T(8,128)S(1)} %bitcast.633, f32[16,128]{1,0:T(8,128)S(1)} %copy-done.9), kind=kLoop, calls=%fused_computation.189 | loop fusion | flops 524288 | bytes 4202496 | tf_op jit(solution)/shard_map/mul | solution.py:45
  91.4 185.2 %while.112 = (s32[]{:T(128)}, f32[16,16,128]{2,0,1:T(8,128)S(1)}, f32[16,1,128]{2,0,1:T(8,128)S(1)}, f32[16,16,16,128]{3,0,1,2:T(8,128)}, f32[16,1,16,128]{3,0,2...) while((s32[]{:T(128)}, f32[16,16,128]{2,0,1:T(8,128)S(1)}, ...), condition=%wide.region_1.2_spmd, body=%wide.region_0.1_spmd.sunk | while | flops 8890370 | bytes 15271725 | solution.py:71
  282.3 249.5 %while.113 = (s32[]{:T(128)}, f32[16,16,128]{2,0,1:T(8,128)S(1)}, f32[16,1,128]{2,0,1:T(8,128)S(1)}, f32[16,16,16,128]{3,2,1,0:T(8,128)}, f32[16,1,16,128]{3,0,2...) while((s32[]{:T(128)}, f32[16,16,128]{2,0,1:T(8,128)S(1)}, ...), condition=%wide.region_3.4_spmd, body=%wide.region_2.3_spmd.sunk | while | flops 8890370 | bytes 15926577 | solution.py:71
  293.3 4.5 dynamic_update_slice.80
  324.5 4.5 dynamic_update_slice.80
  340.1 4.5 dynamic_update_slice.80
  355.7 4.5 dynamic_update_slice.80
  371.2 4.5 dynamic_update_slice.80
  418.1 4.5 dynamic_update_slice.80
  433.7 4.5 dynamic_update_slice.80
  449.3 4.5 dynamic_update_slice.80
  464.9 4.5 dynamic_update_slice.80
  480.5 4.5 dynamic_update_slice.80
  496.0 4.5 dynamic_update_slice.80
  511.6 4.5 dynamic_update_slice.80
  527.2 4.5 dynamic_update_slice.80
  531.8 23.7 %while.115 = (s32[]{:T(128)}, f32[16,1,128]{2,0,1:T(8,128)S(1)}, f32[16,1,16,128]{3,2,1,0:T(8,128)S(1)}, f32[16,1,16,128]{3,0,2,1:T(8,128)S(1)}, f32[16,16,16,12...) while((s32[]{:T(128)}, f32[16,1,128]{2,0,1:T(8,128)S(1)}, ...), condition=%wide.region_5.6_spmd.clone, body=%wide.region_4.5_spmd.clone.sunk | while | flops 67591 | bytes 467105 | solution.py:85
  560.0 23.4 %while.114 = (s32[]{:T(128)}, f32[16,1,128]{2,0,1:T(8,128)S(1)}, f32[16,1,16,128]{3,2,1,0:T(8,128)S(1)}, f32[16,1,16,128]{3,0,2,1:T(8,128)S(1)}, f32[16,16,16,12...) while((s32[]{:T(128)}, f32[16,1,128]{2,0,1:T(8,128)S(1)}, ...), condition=%wide.region_7.8_spmd, body=%wide.region_6.7_spmd.sunk | while | flops 65542 | bytes 450711 | solution.py:85
  (3693 shorter events, 426.9 us)
Async XLA Ops:
  0.0 27.0 %copy-start.14 = (s32[1,128]{1,0:T(1,128)S(1)}, s32[1,128]{1,0:T(1,128)}, u32[]{:S(2)}) copy-start(s32[1,128]{1,0:T(1,128)} %param.85) | copy-start | bytes 1540
  1.0 88.0 %collective-permute-start = (f32[16,16,1,128]{3,0,1,2:T(8,128)S(1)}, f32[16,16,1,128]{3,0,1,2:T(8,128)}, u32[]{:S(2)}, u32[]{:S(2)}) collective-permute-start(f32[16,16,1,128]{3,0,1,2:T(8,128)S(1)} %copy.131), channel_id=1, source_target_pairs={{0,1},{1,2},{2,3},{3,4},{4,5},{5,6},{6,7},{7,8},{8,9},{9,10},{10,1... | collective-permute-start | bytes 393224 | tf_op jit(solution)/shard_map/ppermute | solution.py:14
  7.3 81.7 %collective-permute-start.1 = (f32[16,16,1,128]{3,0,1,2:T(8,128)S(1)}, f32[16,16,1,128]{3,0,1,2:T(8,128)}, u32[]{:S(2)}, u32[]{:S(2)}) collective-permute-start(f32[16,16,1,128]{3,0,1,2:T(8,128)S(1)} %copy.131), channel_id=1, source_target_pairs={{1,0},{2,1},{3,2},{4,3},{5,4},{6,5},{7,6},{8,7},{9,8},{10,9},{11,1... | collective-permute-start | bytes 393224 | tf_op jit(solution)/shard_map/ppermute | solution.py:17
  9.9 19.0 %copy-start = (f32[4,16,16,1,128]{4,3,2,1,0:T(1,128)S(1)}, f32[4,16,16,1,128]{4,3,2,1,0:T(1,128)}, u32[]{:S(2)}) copy-start(f32[4,16,16,1,128]{4,3,2,1,0:T(1,128)} %param.84) | copy-start | bytes 1572868
  11.0 18.7 %copy-start.11 = (s32[1,128]{1,0:T(1,128)S(1)}, s32[1,128]{1,0:T(1,128)}, u32[]{:S(2)}) copy-start(s32[1,128]{1,0:T(1,128)} %param.86) | copy-start | bytes 1540
  11.0 79.4 %all-to-all-start = ((f32[128,16,1,128]{3,1,2,0:T(8,128)}), f32[128,16,1,128]{3,1,2,0:T(8,128)S(1)}, u32[]{:S(2)}, u32[]{:S(2)}) async-start(f32[128,16,1,128]{3,1,2,0:T(8,128)} %stack.3), calls=%async_computation | async-start | bytes 2097152 | tf_op jit(solution)/shard_map/all_to_all | solution.py:109
  62.1 4.3 copy-start.10
  62.1 19.4 %slice-start = ((s8[16777216]{0:T(1024)(128)(4,1)}), s8[4194304]{0:T(1024)(128)(4,1)S(1)}, s32[]{:S(2)}) async-start(s8[16777216]{0:T(1024)(128)(4,1)} %bitcast.632), calls=%async_computation.1 | async-start | bytes 8388608
  66.4 15.1 %slice-start.1 = ((s8[16777216]{0:T(1024)(128)(4,1)}), s8[4194304]{0:T(1024)(128)(4,1)S(1)}, s32[]{:S(2)}) async-start(s8[16777216]{0:T(1024)(128)(4,1)} %bitcast.632), calls=%async_computation.2 | async-start | bytes 8388608
  66.4 15.1 %slice-start.2 = ((s8[16777216]{0:T(1024)(128)(4,1)}), s8[4194304]{0:T(1024)(128)(4,1)S(1)}, s32[]{:S(2)}) async-start(s8[16777216]{0:T(1024)(128)(4,1)} %bitcast.632), calls=%async_computation.3 | async-start | bytes 8388608
  66.4 15.1 %slice-start.3 = ((s8[16777216]{0:T(1024)(128)(4,1)}), s8[4194304]{0:T(1024)(128)(4,1)S(1)}, s32[]{:S(2)}) async-start(s8[16777216]{0:T(1024)(128)(4,1)} %bitcast.632), calls=%async_computation.4 | async-start | bytes 8388608
  66.4 15.1 %copy-start.9 = (f32[16,128]{1,0:T(8,128)S(1)}, f32[16,128]{1,0:T(8,128)}, u32[]{:S(2)}) copy-start(f32[16,128]{1,0:T(8,128)} %get-tuple-element.1778) | copy-start | bytes 24580
  81.5 6.6 %copy-start.15 = (s32[1,128]{1,0:T(1,128)S(1)}, s32[1,128]{1,0:T(1,128)}, u32[]{:S(2)}) copy-start(s32[1,128]{1,0:T(1,128)} %param.87) | copy-start | bytes 1540
  81.5 7.5 %copy-start.13 = (s32[128]{0:T(128)S(1)}, s32[128]{0:T(128)}, u32[]{:S(2)}) copy-start(s32[128]{0:T(128)} %fusion.21) | copy-start | bytes 1540
  81.5 7.5 %copy-start.1 = (f32[16,16,1,1]{3,0,1,2:T(8,128)S(1)}, f32[16,16,1,1]{3,0,1,2:T(8,128)}, u32[]{:S(2)}) copy-start(f32[16,16,1,1]{3,0,1,2:T(8,128)} %get-tuple-element.1776) | copy-start | bytes 3076
  81.5 7.5 %copy-start.2 = (f32[16,16,1,1]{3,0,1,2:T(8,128)S(1)}, f32[16,16,1,1]{3,0,1,2:T(8,128)}, u32[]{:S(2)}) copy-start(f32[16,16,1,1]{3,0,1,2:T(8,128)} %get-tuple-element.1777) | copy-start | bytes 3076
  81.5 7.5 %copy-start.3 = (f32[1,16,16,1,128]{4,3,2,1,0:T(1,128)S(1)}, f32[1,16,16,1,128]{4,3,2,1,0:T(1,128)}, u32[]{:S(2)}) copy-start(f32[1,16,16,1,128]{4,3,2,1,0:T(1,128)} %get-tuple-element.1770) | copy-start | bytes 393220
  81.5 7.5 %copy-start.4 = (f32[1,16,16,1,128]{4,3,2,1,0:T(1,128)S(1)}, f32[1,16,16,1,128]{4,3,2,1,0:T(1,128)}, u32[]{:S(2)}) copy-start(f32[1,16,16,1,128]{4,3,2,1,0:T(1,128)} %get-tuple-element.1771) | copy-start | bytes 393220
  81.6 7.5 %copy-start.5 = (f32[1,16,16,1,128]{4,3,2,1,0:T(1,128)S(1)}, f32[1,16,16,1,128]{4,3,2,1,0:T(1,128)}, u32[]{:S(2)}) copy-start(f32[1,16,16,1,128]{4,3,2,1,0:T(1,128)} %get-tuple-element.1772) | copy-start | bytes 393220
  81.6 7.5 %copy-start.6 = (f32[1,16,16,1,128]{4,3,2,1,0:T(1,128)S(1)}, f32[1,16,16,1,128]{4,3,2,1,0:T(1,128)}, u32[]{:S(2)}) copy-start(f32[1,16,16,1,128]{4,3,2,1,0:T(1,128)} %get-tuple-element.1773) | copy-start | bytes 393220
  81.6 7.5 %copy-start.7 = (f32[16,16,1,128]{3,2,1,0:T(1,128)S(1)}, f32[16,16,1,128]{3,2,1,0:T(1,128)}, u32[]{:S(2)}) copy-start(f32[16,16,1,128]{3,2,1,0:T(1,128)} %param.82) | copy-start | bytes 393220
  81.6 9.5 %copy-start.12 = (pred[128]{0:T(512)(128)(4,1)S(1)}, pred[128]{0:T(512)(128)(4,1)}, u32[]{:S(2)}) copy-start(pred[128]{0:T(512)(128)(4,1)} %compare_and_fusion) | copy-start | bytes 388
  277.6 4.7 collective-permute-start.2
  555.4 4.6 collective-permute-start.3
  (1 other events, 0.7 us)
